TPU v7x, 256 devices: a whole 4x4x8 slice. The times are simulated.
256 devices in a mesh: dp: 32 (over x_lo, z, core), tensor: 8 (over y, x_hi).
Axes of the slice: x: 4 (x_hi: 2, x_lo: 2; x = x_hi * 2 + x_lo), y: 4, z: 8, core: 2. Of those that a mesh axis runs over, the one named last changes fastest.
Arguments:
- tokens: bfloat16 [6144, 2048], P(('dp', 'tensor')), may hold values from -6 to 6
- grad_hidden: bfloat16 [6144, 5504], P('dp', 'tensor'), may hold values from -0.078125 to 0.078125
- width_in: bfloat16 [2048, 1024], P(None, 'tensor'), may hold values from -0.125 to 0.125
- gate_small: bfloat16 [1024, 2752], P(None, 'tensor'), may hold values from -0.1875 to 0.1875
- up_small: bfloat16 [1024, 2752], P(None, 'tensor'), may hold values from -0.1875 to 0.1875
- width_hidden: bfloat16 [5504, 2752], P('tensor'), may hold values from -0.109375 to 0.109375
Outputs:
- grad_width_in: float32 [2048, 1024], P('dp', 'tensor')
- grad_gate_small: float32 [1024, 2752], P('dp', 'tensor')
- grad_up_small: float32 [1024, 2752], P('dp', 'tensor')
- grad_width_hidden: float32 [5504, 2752], P('tensor', 'dp')
All inputs are finite; a program needn't handle non-finite values.
Results may differ from a plain program's by a relative error of at most 0.0085.
Values may be sent and summed in bfloat16 or wider, within the bound.
No kernel may reach another device: no remote copies, remote signals or barrier semaphores. Data moves between devices by JAX's collectives and lax.ppermute only.
A program may use at most 64 MiB of HBM per device.

v0:
```python
import jax
import jax.numpy as jnp
from jax import lax
from jax.sharding import PartitionSpec as P


def contract_rows(left, right):
    return lax.dot_general(
        left, right, (((0,), (0,)), ((), ())), preferred_element_type=jnp.float32
    )


def contract_cols(left, right):
    return lax.dot_general(
        left, right, (((1,), (1,)), ((), ())), preferred_element_type=jnp.float32
    )


def on_device(tokens, grad_hidden, width_in, gate_small, up_small, width_hidden):
    all_tokens = lax.all_gather(tokens, "tensor", axis=0, tiled=True)
    narrow_part = jnp.dot(all_tokens, width_in, preferred_element_type=jnp.float32).astype(
        jnp.bfloat16
    )
    narrow = lax.all_gather(narrow_part, "tensor", axis=1, tiled=True)
    gate_part = jnp.dot(narrow, gate_small, preferred_element_type=jnp.float32).astype(jnp.bfloat16)
    up_part = jnp.dot(narrow, up_small, preferred_element_type=jnp.float32).astype(jnp.bfloat16)
    gate_low, up_low = (
        lax.all_gather(gate_part, "tensor", axis=1, tiled=True),
        lax.all_gather(up_part, "tensor", axis=1, tiled=True),
    )
    gate_big = contract_cols(gate_low, width_hidden)
    up_big = contract_cols(up_low, width_hidden)
    upstream = grad_hidden.astype(jnp.float32)
    sig = jax.nn.sigmoid(gate_big)
    d_gate = (upstream * up_big * sig * (1.0 + gate_big * (1.0 - sig))).astype(jnp.bfloat16)
    d_up = (upstream * gate_big * sig).astype(jnp.bfloat16)
    hidden_term = contract_rows(gate_low, d_gate) + contract_rows(up_low, d_up)
    hidden_owned = lax.psum_scatter(hidden_term, "dp", scatter_dimension=0, tiled=True)
    gate_back = jnp.dot(d_gate, width_hidden, preferred_element_type=jnp.float32)
    up_back = jnp.dot(d_up, width_hidden, preferred_element_type=jnp.float32)
    gate_back_own, up_back_own = (
        lax.psum_scatter(gate_back, "tensor", scatter_dimension=1, tiled=True),
        lax.psum_scatter(up_back, "tensor", scatter_dimension=1, tiled=True),
    )
    d_gate_low = gate_back_own.astype(jnp.bfloat16)
    d_up_low = up_back_own.astype(jnp.bfloat16)
    gate_term = contract_rows(narrow, d_gate_low)
    up_term = contract_rows(narrow, d_up_low)
    grad_gate_small, grad_up_small = (
        lax.psum_scatter(gate_term, "dp", scatter_dimension=0, tiled=True),
        lax.psum_scatter(up_term, "dp", scatter_dimension=0, tiled=True),
    )
    narrow_back = contract_cols(d_gate_low, gate_small) + contract_cols(d_up_low, up_small)
    d_narrow = lax.psum_scatter(narrow_back, "tensor", scatter_dimension=1, tiled=True).astype(
        jnp.bfloat16
    )
    input_term = contract_rows(all_tokens, d_narrow)
    grad_width_in = lax.psum_scatter(input_term, "dp", scatter_dimension=0, tiled=True)
    return (grad_width_in, grad_gate_small, grad_up_small, hidden_owned.T)


def solution(mesh):
    return jax.shard_map(
        on_device,
        mesh=mesh,
        in_specs=(
            P(("dp", "tensor"), None),
            P("dp", "tensor"),
            P(None, "tensor"),
            P(None, "tensor"),
            P(None, "tensor"),
            P("tensor", None),
        ),
        out_specs=(P("dp", "tensor"), P("dp", "tensor"), P("dp", "tensor"), P("tensor", "dp")),
        check_vma=False,
    )
```

profile of v0, /device:TPU:8, one launch (start us, length us, event | category | flops | bytes accessed | tf_op | source)
XLA Modules:
  0.0 815.3 jit_solution(11428229200431129447)
XLA Ops:
  7.2 0.0 copy-start
  7.2 0.0 copy-start.2
  7.2 0.0 all-gather.5.cloned.1.call-start
  7.2 36.5 %all_gather.12 = bf16[192,2048]{1,0:T(8,128)(2,1)S(1)} all-gather(bf16[24,2048]{1,0:T(8,128)(2,1)} %param.6), channel_id=1, replica_groups=mesh['dp'=32,'tensor'=8] {'tensor'}, dimensions={0}, use_global_device_ids=true | all-gather | bytes 884736 | tf_op jit(solution)/shard_map/all_gather | solution.py:20
  43.7 1.4 convolution_convert_fusion.2
  45.1 33.1 %all_gather.13 = bf16[192,1024]{1,0:T(8,128)(2,1)S(1)} all-gather(bf16[192,128]{1,0:T(8,128)(2,1)S(1)} %convolution_convert_fusion.2), channel_id=1, replica_groups=mesh['dp'=32,'tensor'=8] {'tensor'}, dimensions={1}, use_global_device_ids=true | all-gather | bytes 442368 | tf_op jit(solution)/shard_map/all_gather | solution.py:24
  78.3 0.0 copy-done.2
  78.3 1.1 fusion.4
  79.4 0.0 all-gather.5.cloned.1.call-update
  79.4 0.0 all-gather.7.cloned.1.call-start
  79.5 0.0 copy-done
  79.5 1.1 fusion.5
  80.6 0.0 all-gather.7.cloned.1.call-update
  80.6 0.0 reduce-scatter.21.cloned.1.call-start
  80.6 52.1 %all-gather.5.cloned.1.call-done = bf16[8,344,192]{1,2,0:T(8,128)(2,1)} async-done(((bf16[1,344,192]{1,2,0:T(8,128)(2,1)}), bf16[8,344,192]{1,2,0:T(8,128)(2,1)}) %all-gather.5.cloned.1.call-update) | async-done | bytes 1056784 | tf_op jit(solution)/shard_map/all_gather | solution.py:29
  132.8 3.0 copy.14
  135.7 2.1 reshape.9
  137.8 48.5 %all-gather.7.cloned.1.call-done = bf16[8,344,192]{1,2,0:T(8,128)(2,1)} async-done(((bf16[1,344,192]{1,2,0:T(8,128)(2,1)}), bf16[8,344,192]{1,2,0:T(8,128)(2,1)}) %all-gather.7.cloned.1.call-update) | async-done | bytes 1056784 | tf_op jit(solution)/shard_map/all_gather | solution.py:28
  186.3 3.0 copy.15
  189.3 2.9 reshape.11
  192.1 3.9 fusion.18
  196.0 0.0 copy-done.1
  196.1 0.0 copy-done.5
  196.1 1.4 fusion.3
  197.5 3.4 convolution_bitcast_fusion.1
  200.8 0.0 reduce-scatter.21.cloned.1.call-update
  200.8 0.0 reduce-scatter.23.cloned.1.call-start
  200.9 5.6 convolution_bitcast_fusion
  206.5 0.0 reduce-scatter.23.cloned.1.call-update
  206.5 0.0 reduce-scatter.15.cloned.1.call-start
  206.6 76.9 %reduce-scatter.21.cloned.1.call-done = f32[344,192]{1,0:T(8,128)} async-done(((f32[2752,192]{1,0:T(8,128)}), f32[344,192]{1,0:T(8,128)}) %reduce-scatter.21.cloned.1.call-update) | async-done | bytes 264208
  283.5 1.1 copy.18
  284.6 1.3 fusion.22
  285.9 84.2 %reduce-scatter.23.cloned.1.call-done = f32[344,192]{1,0:T(8,128)} async-done(((f32[2752,192]{1,0:T(8,128)}), f32[344,192]{1,0:T(8,128)}) %reduce-scatter.23.cloned.1.call-update) | async-done | bytes 264208
  370.2 1.1 copy.20
  371.3 2.6 convolution_add_fusion.1
  373.9 0.0 reduce-scatter.15.cloned.1.call-update
  373.9 0.0 reduce-scatter.17.cloned.1.call-start
  374.0 1.7 fusion.21
  375.7 0.0 reduce-scatter.17.cloned.1.call-update
  375.7 0.0 reduce-scatter.19.cloned.1.call-start
  375.8 1.6 fusion.20
  377.4 0.0 reduce-scatter.19.cloned.1.call-update
  377.4 0.0 copy-start.6
  377.4 0.2 reduce-scatter.25.cloned.1.call-start
  377.6 0.0 copy-start.4
  377.7 2.6 fusion.19
  380.3 0.0 copy-done.6
  380.3 0.0 copy-done.4
  380.3 4.7 convolution_add_fusion
  385.0 65.2 %reduce-scatter.15.cloned.1.call-done = f32[192,128]{1,0:T(8,128)} async-done(((f32[192,1024]{1,0:T(8,128)}), f32[192,128]{1,0:T(8,128)}) %reduce-scatter.15.cloned.1.call-update) | async-done | bytes 98320 | tf_op jit(solution)/shard_map/reduce_scatter | solution.py:54
  450.3 1.2 convolution_bitcast_fusion.2
  451.5 1.3 copy.21
  452.8 0.0 reduce-scatter.25.cloned.1.call-update
  452.9 0.0 copy-start.7
  452.9 83.5 %fusion = f32[88,688]{1,0:T(8,128)S(1)} fusion(f32[2752,688]{1,0:T(8,128)} %convolution_add_fusion), kind=kCustom, calls=%all-reduce-scatter | all-reduce-scatter fusion | flops 1937409 | bytes 7816704
  536.4 1.3 collective-permute-start
  537.7 0.6 dynamic-slice.4
  539.0 0.0 collective-permute-done
  539.0 0.3 concatenate
  539.2 0.7 dynamic-slice_bitcast_fusion
  540.0 32.8 %reduce-scatter.17.cloned.1.call-done = f32[32,344]{1,0:T(8,128)} async-done(((f32[1024,344]{1,0:T(8,128)}), f32[32,344]{1,0:T(8,128)}) %reduce-scatter.17.cloned.1.call-update) | async-done | bytes 44048 | tf_op jit(solution)/shard_map/reduce_scatter | solution.py:50
  572.8 118.3 %reduce-scatter.19.cloned.1.call-done = f32[32,344]{1,0:T(8,128)} async-done(((f32[1024,344]{1,0:T(8,128)}), f32[32,344]{1,0:T(8,128)}) %reduce-scatter.19.cloned.1.call-update) | async-done | bytes 44048 | tf_op jit(solution)/shard_map/reduce_scatter | solution.py:51
  691.1 117.3 %reduce-scatter.25.cloned.1.call-done = f32[64,128]{1,0:T(8,128)} async-done(((f32[2048,128]{1,0:T(8,128)}), f32[64,128]{1,0:T(8,128)}) %reduce-scatter.25.cloned.1.call-update) | async-done | bytes 32784
  (6 shorter events, 0.0 us)
Async XLA Ops:
  7.2 72.3 %copy-start = (bf16[1024,344]{0,1:T(8,128)(2,1)S(1)}, bf16[1024,344]{0,1:T(8,128)(2,1)}, u32[]{:S(2)}) copy-start(bf16[1024,344]{0,1:T(8,128)(2,1)} %param.9) | copy-start | bytes 2113540
  7.2 71.1 %copy-start.2 = (bf16[1024,344]{0,1:T(8,128)(2,1)S(1)}, bf16[1024,344]{0,1:T(8,128)(2,1)}, u32[]{:S(2)}) copy-start(bf16[1024,344]{0,1:T(8,128)(2,1)} %param.10) | copy-start | bytes 2113540
  7.2 125.6 %all-gather.5.cloned.1.call-start = ((), (), s32[]{:S(2)}) async-start(), calls=%async_computation.9 | async-start | bytes 1327104 | tf_op jit(solution)/shard_map/all_gather | solution.py:29
  79.4 106.9 %all-gather.7.cloned.1.call-start = ((), (), s32[]{:S(2)}) async-start(), calls=%async_computation.10 | async-start | bytes 1327104 | tf_op jit(solution)/shard_map/all_gather | solution.py:28
  80.6 202.9 %reduce-scatter.21.cloned.1.call-start = ((), (), s32[]{:S(2)}) async-start(), calls=%async_computation.11 | async-start | bytes 3170304
  192.1 3.9 copy-start.1
  192.1 3.9 copy-start.5
  196.1 1.4 copy-start.3
  200.8 169.3 %reduce-scatter.23.cloned.1.call-start = ((), (), s32[]{:S(2)}) async-start(), calls=%async_computation.12 | async-start | bytes 3170304
  206.5 243.7 %reduce-scatter.15.cloned.1.call-start = ((), (), s32[]{:S(2)}) async-start(), calls=%async_computation.6 | async-start | bytes 884736 | tf_op jit(solution)/shard_map/reduce_scatter | solution.py:54
  373.9 198.8 %reduce-scatter.17.cloned.1.call-start = ((), (), s32[]{:S(2)}) async-start(), calls=%async_computation.7 | async-start | bytes 1622016 | tf_op jit(solution)/shard_map/reduce_scatter | solution.py:50
  375.7 315.4 %reduce-scatter.19.cloned.1.call-start = ((), (), s32[]{:S(2)}) async-start(), calls=%async_computation.8 | async-start | bytes 1622016 | tf_op jit(solution)/shard_map/reduce_scatter | solution.py:51
  377.4 2.9 copy-start.6
  377.4 431.0 %reduce-scatter.25.cloned.1.call-start = ((), (), s32[]{:S(2)}) async-start(), calls=%async_computation.13 | async-start | bytes 1081344
  377.6 2.7 copy-start.4
  452.9 84.9 %copy-start.7 = (u32[256]{0:T(256)S(1)}, u32[256]{0:T(256)}, u32[]{:S(2)}) copy-start(u32[256]{0:T(256)} %constant.5) | copy-start | bytes 3076
  536.4 2.6 collective-permute-start
Sparse Core Ops, SparseCore 0:
  79.5 53.1 all-gather.4
  135.3 50.8 all-gather.6
  201.0 82.5 reduce-scatter.20
  287.5 82.6 reduce-scatter.22
  374.1 76.1 reduce-scatter.14
  453.2 119.5 reduce-scatter.16
  575.9 115.2 reduce-scatter.18
  694.2 114.1 reduce-scatter.24
where the time goes:
time: 816 us; the launch traced here: 815 us
  waiting for transfers between devices  596 us (73%)
  blocking collectives  153 us (19%)
  matrix products  33.6 us (4%)
  local copies, waits for them, and re-layouts  16.1 us (2%)
  between operations  15 us (2%)
    unnamed x12, waiting for transfers between devices  279 us
    reduce_scatter x1, waiting for transfers between devices, on_device(): lax.psum_scatter(up_term, 'dp', scatter_dimension=0, tiled=True)  118 us
    unnamed x1, blocking collectives  83.5 us
    reduce_scatter x1, waiting for transfers between devices, on_device(): lax.psum_scatter(narrow_back, 'tensor', scatter_dimension=1, tiled=True)  65.2 us
    all_gather x1, waiting for transfers between devices, on_device(): lax.all_gather(up_part, 'tensor', axis=1, tiled=True)  52.1 us
    all_gather x1, waiting for transfers between devices, on_device(): lax.all_gather(gate_part, 'tensor', axis=1, tiled=True)  48.5 us
    all_gather x1, blocking collectives, on_device(): all_tokens = lax.all_gather(tokens, 'tensor', axis=0, tiled=True)  36.5 us
    all_gather x1, blocking collectives, on_device(): narrow = lax.all_gather(narrow_part, 'tensor', axis=1, tiled=True)  33.1 us
  transfers between devices with their start and end apart: 9, of which 8 were waited for; matrix products, arithmetic and copies ran while one was open for 14% of the time, Pallas kernels for 0%

commit v1 on v0

--- a/solution.py
+++ b/solution.py
@@ -2,6 +2,13 @@
 import jax.numpy as jnp
 from jax import lax
 from jax.sharding import PartitionSpec as P
+
+
+def swapped_in(x, mesh_axis, dim):
+    size = lax.axis_size(mesh_axis)
+    shards = jnp.stack([x for _ in range(size)])
+    shards = lax.all_to_all(shards, mesh_axis, split_axis=0, concat_axis=0)
+    return jnp.concatenate(shards, axis=dim)
 
 
 def contract_rows(left, right):
@@ -26,7 +33,7 @@
     up_part = jnp.dot(narrow, up_small, preferred_element_type=jnp.float32).astype(jnp.bfloat16)
     gate_low, up_low = (
         lax.all_gather(gate_part, "tensor", axis=1, tiled=True),
-        lax.all_gather(up_part, "tensor", axis=1, tiled=True),
+        swapped_in(up_part, "tensor", 1),
     )
     gate_big = contract_cols(gate_low, width_hidden)
     up_big = contract_cols(up_low, width_hidden)

time: 816 us -> 762 us (0.934)
  waiting for transfers between devices: 596 us -> 526 us
  blocking collectives: 153 us -> 172 us
    all_gather x1 -> x0, waiting for transfers between devices: 52.1 us -> none  [on_device(): lax.all_gather(up_part, 'tensor', axis=1, tiled=True)]
    all_to_all x0 -> x1, blocking collectives: none -> 18.4 us  [swapped_in(): shards = lax.all_to_all(shards, mesh_axis, split_axis=0, concat_axis=0)]
    all_gather x1, waiting for transfers between devices: 48.5 us -> 30.9 us  [on_device(): lax.all_gather(gate_part, 'tensor', axis=1, tiled=True)]
    unnamed x12 -> x11, waiting for transfers between devices: 279 us -> 279 us
  transfers between devices with their start and end apart: 9 -> 8, of which waited for: 8 -> 7; matrix products, arithmetic and copies ran while one was open for 14% -> 15% of each run, Pallas kernels for 0% -> 0%
where the time goes in v1:
time: 762 us
  waiting for transfers between devices  526 us (69%)
  blocking collectives  172 us (23%)
  matrix products  32.9 us (4%)
  local copies, waits for them, and re-layouts  15 us (2%)
  between operations  15 us (2%)
    unnamed x11, waiting for transfers between devices  279 us
    reduce_scatter x1, waiting for transfers between devices, on_device(): lax.psum_scatter(up_term, 'dp', scatter_dimension=0, tiled=True)  118 us
    unnamed x1, blocking collectives  83.5 us
    reduce_scatter x1, waiting for transfers between devices, on_device(): lax.psum_scatter(narrow_back, 'tensor', scatter_dimension=1, tiled=True)  65.2 us
    all_gather x1, blocking collectives, on_device(): all_tokens = lax.all_gather(tokens, 'tensor', axis=0, tiled=True)  36.5 us
    all_gather x1, blocking collectives, on_device(): narrow = lax.all_gather(narrow_part, 'tensor', axis=1, tiled=True)  33.2 us
    reduce_scatter x1, waiting for transfers between devices, on_device(): lax.psum_scatter(gate_term, 'dp', scatter_dimension=0, tiled=True)  32.7 us
    all_gather x1, waiting for transfers between devices, on_device(): lax.all_gather(gate_part, 'tensor', axis=1, tiled=True)  30.9 us
  transfers between devices with their start and end apart: 8, of which 7 were waited for; matrix products, arithmetic and copies ran while one was open for 15% of the time, Pallas kernels for 0%

profile of v1, /device:TPU:8, one launch (start us, length us, event | category | flops | bytes accessed | tf_op | source)
XLA Modules:
  0.0 762.0 jit_solution(13947187883937684502)
XLA Ops:
  7.2 0.0 copy-start
  7.2 0.0 copy-start.2
  7.2 0.0 all-gather.3.cloned.1.call-start
  7.2 36.5 %all_gather.9 = bf16[192,2048]{1,0:T(8,128)(2,1)S(1)} all-gather(bf16[24,2048]{1,0:T(8,128)(2,1)} %param.6), channel_id=1, replica_groups=mesh['dp'=32,'tensor'=8] {'tensor'}, dimensions={0}, use_global_device_ids=true | all-gather | bytes 884736 | tf_op jit(solution)/shard_map/all_gather | solution.py:27
  43.7 1.4 convolution_convert_fusion.2
  45.1 33.2 %all_gather.10 = bf16[192,1024]{1,0:T(8,128)(2,1)S(1)} all-gather(bf16[192,128]{1,0:T(8,128)(2,1)S(1)} %convolution_convert_fusion.2), channel_id=1, replica_groups=mesh['dp'=32,'tensor'=8] {'tensor'}, dimensions={1}, use_global_device_ids=true | all-gather | bytes 442368 | tf_op jit(solution)/shard_map/all_gather | solution.py:31
  78.4 0.0 copy-done
  78.4 1.1 fusion.4
  79.5 0.0 all-gather.3.cloned.1.call-update
  79.5 0.0 reduce-scatter.21.cloned.1.call-start
  79.5 0.0 copy-done.2
  79.5 0.4 convolution_convert_fusion.1
  80.0 0.1 stack.2
  80.1 18.4 %all_to_all.5 = bf16[8,192,344]{2,1,0:T(8,128)(2,1)S(1)} all-to-all(bf16[8,192,344]{2,1,0:T(8,128)(2,1)S(1)} %stack.2), channel_id=1, replica_groups=mesh['dp'=32,'tensor'=8] {'tensor'}, dimensions={0} | all-to-all | bytes 2113536 | tf_op jit(solution)/shard_map/all_to_all | solution.py:10
  98.5 1.7 copy.13
  100.2 2.1 reshape.17
  102.3 30.9 %all-gather.3.cloned.1.call-done = bf16[8,344,192]{1,2,0:T(8,128)(2,1)} async-done(((bf16[1,344,192]{1,2,0:T(8,128)(2,1)}), bf16[8,344,192]{1,2,0:T(8,128)(2,1)}) %all-gather.3.cloned.1.call-update) | async-done | bytes 1056784 | tf_op jit(solution)/shard_map/all_gather | solution.py:35
  133.2 3.0 copy.14
  136.2 2.9 reshape.19
  139.0 3.9 fusion.17
  142.9 0.0 copy-done.1
  142.9 0.0 copy-done.5
  142.9 0.0 copy-start.3
  143.0 1.4 fusion.3
  144.3 0.0 copy-done.3
  144.3 3.4 convolution_bitcast_fusion.1
  147.7 0.0 reduce-scatter.21.cloned.1.call-update
  147.7 0.0 reduce-scatter.23.cloned.1.call-start
  147.8 5.6 convolution_bitcast_fusion
  153.4 0.0 reduce-scatter.23.cloned.1.call-update
  153.4 0.0 reduce-scatter.15.cloned.1.call-start
  153.5 77.0 %reduce-scatter.21.cloned.1.call-done = f32[344,192]{1,0:T(8,128)} async-done(((f32[2752,192]{1,0:T(8,128)}), f32[344,192]{1,0:T(8,128)}) %reduce-scatter.21.cloned.1.call-update) | async-done | bytes 264208
  230.4 1.1 copy.17
  231.6 1.3 fusion.21
  232.8 84.3 %reduce-scatter.23.cloned.1.call-done = f32[344,192]{1,0:T(8,128)} async-done(((f32[2752,192]{1,0:T(8,128)}), f32[344,192]{1,0:T(8,128)}) %reduce-scatter.23.cloned.1.call-update) | async-done | bytes 264208
  317.1 1.1 copy.19
  318.2 2.6 convolution_add_fusion.1
  320.9 0.0 reduce-scatter.15.cloned.1.call-update
  320.9 0.0 reduce-scatter.17.cloned.1.call-start
  320.9 1.7 fusion.20
  322.6 0.0 reduce-scatter.17.cloned.1.call-update
  322.6 0.0 reduce-scatter.19.cloned.1.call-start
  322.7 1.6 fusion.19
  324.3 0.0 reduce-scatter.19.cloned.1.call-update
  324.3 0.0 copy-start.6
  324.4 0.2 reduce-scatter.25.cloned.1.call-start
  324.6 0.0 copy-start.4
  324.6 2.6 fusion.18
  327.3 4.7 convolution_add_fusion
  331.9 65.2 %reduce-scatter.15.cloned.1.call-done = f32[192,128]{1,0:T(8,128)} async-done(((f32[192,1024]{1,0:T(8,128)}), f32[192,128]{1,0:T(8,128)}) %reduce-scatter.15.cloned.1.call-update) | async-done | bytes 98320 | tf_op jit(solution)/shard_map/reduce_scatter | solution.py:61
  397.2 1.2 convolution_bitcast_fusion.2
  398.4 1.3 copy.20
  399.7 0.0 reduce-scatter.25.cloned.1.call-update
  399.8 0.0 copy-start.7
  399.8 83.5 %fusion = f32[88,688]{1,0:T(8,128)S(1)} fusion(f32[2752,688]{1,0:T(8,128)} %convolution_add_fusion), kind=kCustom, calls=%all-reduce-scatter | all-reduce-scatter fusion | flops 1937409 | bytes 7816704
  483.3 1.3 collective-permute-start
  484.6 0.0 copy-done.7
  484.6 0.6 dynamic-slice.4
  485.9 0.0 collective-permute-done
  485.9 0.3 concatenate
  486.2 0.7 dynamic-slice_bitcast_fusion
  486.9 32.7 %reduce-scatter.17.cloned.1.call-done = f32[32,344]{1,0:T(8,128)} async-done(((f32[1024,344]{1,0:T(8,128)}), f32[32,344]{1,0:T(8,128)}) %reduce-scatter.17.cloned.1.call-update) | async-done | bytes 44048 | tf_op jit(solution)/shard_map/reduce_scatter | solution.py:57
  519.6 117.8 %reduce-scatter.19.cloned.1.call-done = f32[32,344]{1,0:T(8,128)} async-done(((f32[1024,344]{1,0:T(8,128)}), f32[32,344]{1,0:T(8,128)}) %reduce-scatter.19.cloned.1.call-update) | async-done | bytes 44048 | tf_op jit(solution)/shard_map/reduce_scatter | solution.py:58
  637.4 117.7 %reduce-scatter.25.cloned.1.call-done = f32[64,128]{1,0:T(8,128)} async-done(((f32[2048,128]{1,0:T(8,128)}), f32[64,128]{1,0:T(8,128)}) %reduce-scatter.25.cloned.1.call-update) | async-done | bytes 32784
  (5 shorter events, 0.0 us)
Async XLA Ops:
  7.2 71.2 %copy-start = (bf16[1024,344]{0,1:T(8,128)(2,1)S(1)}, bf16[1024,344]{0,1:T(8,128)(2,1)}, u32[]{:S(2)}) copy-start(bf16[1024,344]{0,1:T(8,128)(2,1)} %param.9) | copy-start | bytes 2113540
  7.2 72.4 %copy-start.2 = (bf16[1024,344]{0,1:T(8,128)(2,1)S(1)}, bf16[1024,344]{0,1:T(8,128)(2,1)}, u32[]{:S(2)}) copy-start(bf16[1024,344]{0,1:T(8,128)(2,1)} %param.10) | copy-start | bytes 2113540
  7.2 126.0 %all-gather.3.cloned.1.call-start = ((), (), s32[]{:S(2)}) async-start(), calls=%async_computation.10 | async-start | bytes 1327104 | tf_op jit(solution)/shard_map/all_gather | solution.py:35
  79.5 150.9 %reduce-scatter.21.cloned.1.call-start = ((), (), s32[]{:S(2)}) async-start(), calls=%async_computation.11 | async-start | bytes 3170304
  139.0 3.9 copy-start.1
  139.0 3.9 copy-start.5
  142.9 1.4 copy-start.3
  147.7 169.4 %reduce-scatter.23.cloned.1.call-start = ((), (), s32[]{:S(2)}) async-start(), calls=%async_computation.12 | async-start | bytes 3170304
  153.4 243.8 %reduce-scatter.15.cloned.1.call-start = ((), (), s32[]{:S(2)}) async-start(), calls=%async_computation.7 | async-start | bytes 884736 | tf_op jit(solution)/shard_map/reduce_scatter | solution.py:61
  320.9 198.7 %reduce-scatter.17.cloned.1.call-start = ((), (), s32[]{:S(2)}) async-start(), calls=%async_computation.8 | async-start | bytes 1622016 | tf_op jit(solution)/shard_map/reduce_scatter | solution.py:57
  322.6 314.8 %reduce-scatter.19.cloned.1.call-start = ((), (), s32[]{:S(2)}) async-start(), calls=%async_computation.9 | async-start | bytes 1622016 | tf_op jit(solution)/shard_map/reduce_scatter | solution.py:58
  324.3 2.9 copy-start.6
  324.4 430.8 %reduce-scatter.25.cloned.1.call-start = ((), (), s32[]{:S(2)}) async-start(), calls=%async_computation.13 | async-start | bytes 1081344
  324.6 2.7 copy-start.4
  399.8 84.9 %copy-start.7 = (u32[256]{0:T(256)S(1)}, u32[256]{0:T(256)}, u32[]{:S(2)}) copy-start(u32[256]{0:T(256)} %constant.5) | copy-start | bytes 3076
  483.3 2.6 collective-permute-start
Sparse Core Ops, SparseCore 0:
  79.6 53.5 all-gather.2
  147.8 82.5 reduce-scatter.20
  234.5 82.5 reduce-scatter.22
  321.0 76.1 reduce-scatter.14
  400.1 119.4 reduce-scatter.16
  522.5 114.8 reduce-scatter.18
  640.5 114.6 reduce-scatter.24
